TPU v7x, 512 devices: a whole 4x8x8 slice. The times are simulated.
512 devices in a mesh: row: 32 (over x, y), col: 16 (over z, core).
Axes of the slice: x: 4, y: 8, z: 8, core: 2. Of those that a mesh axis runs over, the one named last changes fastest.
Arguments:
- amplitudes: bfloat16 [32768, 32768], P('row', 'col'), may hold values from -6 to 6
- integrals: bfloat16 [32768, 1024], P('col', 'row'), may hold values from -0.03125 to 0.03125
- tile_mask: int32 [256, 256], P('row', 'col'), may hold values 0 or 1
Outputs:
- residual: bfloat16 [32768, 1024], P('row', 'col')
All inputs are finite; a program needn't handle non-finite values. No bound on the sum of `tile_mask` on one device may be relied on, other than what follows from the above.
Results may differ from a plain program's by a relative error of at most 0.001.
Values may be sent and summed in bfloat16 or wider, within the bound.
A program may use at most 64 MiB of HBM per device.

v0:
```python
import jax
import jax.numpy as jnp
from jax import lax
from jax.sharding import PartitionSpec as P


def apply_mask(amplitudes, tile_mask):
    tiles_m, tiles_k = tile_mask.shape
    tile_rows = amplitudes.shape[0] // tiles_m
    tile_cols = amplitudes.shape[1] // tiles_k
    blocks = amplitudes.reshape(tiles_m, tile_rows, tiles_k, tile_cols)
    weights = tile_mask.astype(amplitudes.dtype)[:, None, :, None]
    return (blocks * weights).reshape(amplitudes.shape)


def per_device(amplitudes, integrals, tile_mask):
    masked = apply_mask(amplitudes, tile_mask)
    partial_sums = jnp.dot(
        masked,
        lax.all_gather(integrals, "row", axis=1, tiled=True),
        preferred_element_type=jnp.float32,
    )
    summed = lax.psum_scatter(partial_sums, "col", scatter_dimension=1, tiled=True)
    return summed.astype(jnp.bfloat16)


def solution(mesh):
    placed = (P("row", "col"), P("col", "row"), P("row", "col"))
    return jax.shard_map(
        per_device, mesh=mesh, in_specs=placed, out_specs=P("row", "col"), check_vma=False
    )
```

profile of v0, /device:TPU:2, one launch (start us, length us, event | category | flops | bytes accessed | tf_op | source)
XLA Modules:
  0.0 185.4 jit_solution(4674022924054727534)
XLA Ops:
  6.5 0.0 all-gather.2.cloned.1.call-start
  6.5 0.7 all-gather.2.cloned.1.call-update
  7.3 0.0 reduce-scatter.2.cloned.1.call-start
  7.3 0.7 convert_element_type.6
  8.0 92.9 %all-gather.2.cloned.1.call-done = bf16[2048,1024]{0,1:T(8,128)(2,1)} async-done(((bf16[2048,32]{0,1:T(8,128)(2,1)}), bf16[2048,1024]{0,1:T(8,128)(2,1)}) %all-gather.2.cloned.1.call-update) | async-done | bytes 4194320 | tf_op jit(solution)/shard_map/all_gather | solution.py:20
  100.9 0.0 copy-start
  100.9 0.6 mul.11
  101.5 1.6 copy-done
  103.0 8.5 %fusion = f32[1024,1024]{0,1:T(8,128)} fusion(bf16[2048,1024]{0,1:T(8,128)(2,1)} %all-gather.2.cloned.1.call-done, bf16[1024,2048]{1,0:T(8,128)(2,1)S(1)} %copy-done, bf16[128,8,16,128]{3,2,1,0:T(8,128)(2,1)S(1)} %bitcast.6), kind=kOutput, calls=%fused_computation.1 | convolution fusion | flops 4297064448 | bytes 16777216 | tf_op jit(solution)/shard_map/dot_general | solution.py:18
  111.6 0.0 reduce-scatter.2.cloned.1.call-update
  111.6 65.3 %reduce-scatter.2.cloned.1.call-done = f32[1024,64]{0,1:T(8,128)} async-done(((f32[1024,1024]{0,1:T(8,128)}), f32[1024,64]{0,1:T(8,128)}) %reduce-scatter.2.cloned.1.call-update) | async-done | bytes 262160 | tf_op jit(solution)/shard_map/reduce_scatter | solution.py:23
  176.9 1.6 convert_element_type.7
Async XLA Ops:
  6.5 94.3 %all-gather.2.cloned.1.call-start = ((), (), s32[]{:S(2)}) async-start(), calls=%async_computation.1 | async-start | bytes 4325376 | tf_op jit(solution)/shard_map/all_gather | solution.py:20
  7.3 169.7 %reduce-scatter.2.cloned.1.call-start = ((), (), s32[]{:S(2)}) async-start(), calls=%async_computation.2 | async-start | bytes 4456448 | tf_op jit(solution)/shard_map/reduce_scatter | solution.py:23
  100.9 2.2 %copy-start = (bf16[1024,2048]{1,0:T(8,128)(2,1)S(1)}, bf16[1024,2048]{1,0:T(8,128)(2,1)}, u32[]{:S(2)}) copy-start(bf16[1024,2048]{1,0:T(8,128)(2,1)} %param.3) | copy-start | bytes 12582916
Sparse Core Ops, SparseCore 0:
  10.5 90.2 all-gather.1
  111.7 65.1 reduce-scatter.1
where the time goes:
time: 186 us; the launch traced here: 185 us
  waiting for transfers between devices  159 us (85%)
  between operations  13.4 us (7%)
  matrix products  8.55 us (5%)
  other arithmetic  2.31 us (1%)
  local copies, waits for them, and re-layouts  2.18 us (1%)
    all_gather x1, waiting for transfers between devices, per_device(): lax.all_gather(integrals, 'row', axis=1, tiled=True)  92.9 us
    reduce_scatter x1, waiting for transfers between devices, per_device(): lax.psum_scatter(partial_sums, 'col', scatter_dimension=1, tiled=True)  65.3 us
    dot_general x1, matrix products, per_device(): jnp.dot(masked, lax.all_gather(integrals, 'row', axis=1, tiled=True), pre...  8.55 us
  transfers between devices with their start and end apart: 2, of which 2 were waited for; matrix products, arithmetic and copies ran while one was open for 0% of the time, Pallas kernels for 0%

commit v1 on v0

--- a/solution.py
+++ b/solution.py
@@ -2,6 +2,7 @@
 import jax.numpy as jnp
 from jax import lax
 from jax.sharding import PartitionSpec as P
+from jax.lax import all_to_all, axis_size
 
 
 def apply_mask(amplitudes, tile_mask):
@@ -17,7 +18,7 @@
     masked = apply_mask(amplitudes, tile_mask)
     partial_sums = jnp.dot(
         masked,
-        lax.all_gather(integrals, "row", axis=1, tiled=True),
+        jnp.concatenate(all_to_all(jnp.stack([integrals] * axis_size("row")), "row", 0, 0), axis=1),
         preferred_element_type=jnp.float32,
     )
     summed = lax.psum_scatter(partial_sums, "col", scatter_dimension=1, tiled=True)

time: 186 us -> 203 us (1.091)
  the two profiles are of different devices: /device:TPU:2 before, /device:TPU:8 now
where the time goes in v1:
time: 203 us
  waiting for transfers between devices  163 us (80%)
  between operations  13.4 us (7%)
  starting transfers between devices  10.4 us (5%)
  matrix products  8.57 us (4%)
  local copies, waits for them, and re-layouts  5.57 us (3%)
    all_to_all x1, waiting for transfers between devices, per_device(): all_to_all(jnp.stack([integrals] * axis_size('row')), 'row', 0, 0)  95.1 us
    reduce_scatter x1, waiting for transfers between devices, per_device(): lax.psum_scatter(partial_sums, 'col', scatter_dimension=1, tiled=True)  67.8 us
    all_to_all x1, starting transfers between devices, per_device(): all_to_all(jnp.stack([integrals] * axis_size('row')), 'row', 0, 0)  10.4 us
    dot_general x1, matrix products, per_device(): jnp.dot(masked, jnp.concatenate(all_to_all(jnp.stack([integrals] * axis_s...  8.57 us
  transfers between devices with their start and end apart: 2, of which 2 were waited for; matrix products, arithmetic and copies ran while one was open for 0% of the time, Pallas kernels for 0%

profile of v1, /device:TPU:8, one launch (start us, length us, event | category | flops | bytes accessed | tf_op | source)
XLA Modules:
  0.0 202.5 jit_solution(8389380161461674209)
XLA Ops:
  6.5 3.4 %stack.2 = bf16[32,2048,32]{1,2,0:T(8,128)(2,1)} broadcast(bf16[2048,32]{0,1:T(8,128)(2,1)} %param.4), dimensions={1,2} | broadcast | bytes 4325376 | tf_op jit(solution)/shard_map/stack | solution.py:21
  9.9 0.0 copy-start
  9.9 10.4 %all-to-all-start = ((bf16[32,2048,32]{1,2,0:T(8,128)(2,1)}), bf16[32,2048,32]{1,2,0:T(8,128)(2,1)}, u32[]{:S(2)}, u32[]{:S(2)}) async-start(bf16[32,2048,32]{1,2,0:T(8,128)(2,1)} %stack.2), calls=%async_computation | async-start | bytes 8388608 | tf_op jit(solution)/shard_map/all_to_all | solution.py:21
  20.3 0.0 reduce-scatter.2.cloned.1.call-start
  20.4 0.0 copy-done
  20.4 95.1 %all-to-all-done = bf16[32,2048,32]{1,2,0:T(8,128)(2,1)} async-done(((bf16[32,2048,32]{1,2,0:T(8,128)(2,1)}), bf16[32,2048,32]{1,2,0:T(8,128)(2,1)}, u32[]{:S(2)}, u32[]{:S(2)}) %all-to-all-start) | async-done | bytes 4194336 | tf_op jit(solution)/shard_map/all_to_all | solution.py:21
  115.5 0.0 copy-start.1
  115.5 0.6 mul.11
  116.1 1.6 copy-done.1
  117.7 8.6 %fusion = f32[1024,1024]{0,1:T(8,128)} fusion(bf16[2048,1024]{0,1:T(8,128)(2,1)} %bitcast.1, bf16[1024,2048]{1,0:T(8,128)(2,1)S(1)} %copy-done.1, bf16[128,8,16,128]{3,2,1,0:T(8,128)(2,1)S(1)} %bitcast.9), kind=kOutput, calls=%fused_computation.1 | convolution fusion | flops 4297064448 | bytes 16777216 | tf_op jit(solution)/shard_map/dot_general | solution.py:19
  126.2 0.0 reduce-scatter.2.cloned.1.call-update
  126.3 67.8 %reduce-scatter.2.cloned.1.call-done = f32[1024,64]{0,1:T(8,128)} async-done(((f32[1024,1024]{0,1:T(8,128)}), f32[1024,64]{0,1:T(8,128)}) %reduce-scatter.2.cloned.1.call-update) | async-done | bytes 262160 | tf_op jit(solution)/shard_map/reduce_scatter | solution.py:24
  194.1 1.6 convert_element_type.7
  (1 shorter events, 0.0 us)
Async XLA Ops:
  9.9 10.5 %copy-start = (s32[8,16]{1,0:T(8,128)S(1)}, s32[8,16]{1,0:T(8,128)}, u32[]{:S(2)}) copy-start(s32[8,16]{1,0:T(8,128)} %param.5) | copy-start | bytes 1540
  9.9 105.6 %all-to-all-start = ((bf16[32,2048,32]{1,2,0:T(8,128)(2,1)}), bf16[32,2048,32]{1,2,0:T(8,128)(2,1)}, u32[]{:S(2)}, u32[]{:S(2)}) async-start(bf16[32,2048,32]{1,2,0:T(8,128)(2,1)} %stack.2), calls=%async_computation | async-start | bytes 8388608 | tf_op jit(solution)/shard_map/all_to_all | solution.py:21
  20.3 173.7 %reduce-scatter.2.cloned.1.call-start = ((), (), s32[]{:S(2)}) async-start(), calls=%async_computation.2 | async-start | bytes 4456448 | tf_op jit(solution)/shard_map/reduce_scatter | solution.py:24
  115.5 2.2 %copy-start.1 = (bf16[1024,2048]{1,0:T(8,128)(2,1)S(1)}, bf16[1024,2048]{1,0:T(8,128)(2,1)}, u32[]{:S(2)}) copy-start(bf16[1024,2048]{1,0:T(8,128)(2,1)} %param.3) | copy-start | bytes 12582916
Sparse Core Ops, SparseCore 0:
  126.4 67.6 reduce-scatter.1
